TPU v7x, 32 devices: a whole 2x2x4 slice. The times are simulated.
32 devices in a mesh: seq: 16 (over z, y, x), mp: 2 (over core).
Axes of the slice: x: 2, y: 2, z: 4, core: 2. Of those that a mesh axis runs over, the one named last changes fastest.
Arguments:
- layer_input: bfloat16 [128, 8192], P('seq'), may hold values from -6 to 6
- w_query: bfloat16 [8192, 8192], P('seq', 'mp'), may hold values from -0.0625 to 0.0625
- w_key: bfloat16 [8192, 1024], P('seq', 'mp'), may hold values from -0.1875 to 0.1875
- w_value: bfloat16 [8192, 1024], P('seq', 'mp'), may hold values from -0.0625 to 0.0625
- w_out: bfloat16 [8192, 8192], P('mp', 'seq'), may hold values from -0.0625 to 0.0625
- kv_cache: bfloat16 [2, 32, 4096, 1024], P(None, None, 'seq', 'mp'), may hold values from -180 to 180, as said below
- cache_len: int32 [32], replicated, may hold values from 1 to 4096, as said below
Outputs:
- attn_out: bfloat16 [128, 8192], P('mp', 'seq')
Inputs may be any that keep to these rules, and one draw needn't show every extreme that they name: kv_cache entries at positions at or beyond a request's cache_len are never read. `cache_len`: exactly 4096 for at least one request.
All inputs are finite; a program needn't handle non-finite values.
Results may differ from a plain program's by a relative error of at most 0.012.
The roundings to bfloat16 on the way count: a program that leaves them out, or rounds other values in their place, can miss the bound.
Values may be sent and summed in bfloat16 or wider, within the bound.
A program may use at most 192 MiB of HBM per device.

v0:
```python
import math
import jax
import jax.numpy as jnp
from jax import lax
from jax.sharding import PartitionSpec as P

HD = 128
NEG_FILL = -1e30


def inverse_freq():
    index = jnp.arange(HD // 2, dtype=jnp.float32)
    base_freq = jnp.exp(-(2.0 * index / HD) * math.log(500000.0))
    wavelength = 2.0 * math.pi / base_freq
    smooth = jnp.clip((8192.0 / wavelength - 1.0) / 3.0, 0.0, 1.0)
    return (1.0 - smooth) * base_freq / 8.0 + smooth * base_freq


def rotate(values, positions):
    angles = positions.astype(jnp.float32)[..., None] * inverse_freq()
    cosine = jnp.cos(angles)
    sines = jnp.sin(angles)
    half_width = HD // 2
    first_half = values[..., :half_width]
    second_half = values[..., half_width:]
    return jnp.concatenate(
        [first_half * cosine - second_half * sines, second_half * cosine + first_half * sines],
        axis=-1,
    )


def shards(layer_input, w_query, w_key, w_value, w_out, kv_cache, cache_len):
    widened = layer_input.astype(jnp.float32)
    normed = (
        widened * lax.rsqrt(jnp.mean(widened * widened, axis=-1, keepdims=True) + 1e-05)
    ).astype(jnp.bfloat16)
    gathered = lax.all_to_all(normed, "seq", split_axis=1, concat_axis=0, tiled=True)
    partial_query = jnp.dot(gathered, w_query, preferred_element_type=jnp.float32)
    partial_key = jnp.dot(gathered, w_key, preferred_element_type=jnp.float32)
    partial_value = jnp.dot(gathered, w_value, preferred_element_type=jnp.float32)
    row_count = gathered.shape[0]
    request_count = cache_len.shape[0]
    decode_count = row_count // request_count
    heads_here = partial_query.shape[1] // HD
    kv_here = partial_key.shape[1] // HD
    group_size = heads_here // kv_here
    score_scale = 1.0 / math.sqrt(HD)
    highest = lax.Precision.HIGHEST
    query_all, key_all, value_all = lax.psum((partial_query, partial_key, partial_value), "seq")
    positions = (cache_len[:, None] + jnp.arange(decode_count, dtype=jnp.int32)[None, :]).reshape(
        row_count
    )
    queries = rotate(query_all.reshape(row_count, heads_here, HD), positions[:, None]).astype(
        jnp.bfloat16
    )
    keys_new = rotate(key_all.reshape(row_count, kv_here, HD), positions[:, None]).astype(
        jnp.bfloat16
    )
    values_new = value_all.astype(jnp.bfloat16)
    queries = queries.reshape(request_count, decode_count, kv_here, group_size, HD)
    keys_new = keys_new.reshape(request_count, decode_count, kv_here, HD)
    values_new = values_new.reshape(request_count, decode_count, kv_here, HD)
    block_size = kv_cache.shape[2]
    cache_keys = kv_cache[0].reshape(request_count, block_size, kv_here, HD)
    cache_values = kv_cache[1].reshape(request_count, block_size, kv_here, HD).astype(jnp.float32)
    first_slot = lax.axis_index("seq") * block_size
    slot_index = first_slot + jnp.arange(block_size, dtype=jnp.int32)
    active_slot = (slot_index[None, :] < cache_len[:, None])[:, None, None, None, :]
    causal = (jnp.arange(decode_count)[:, None] >= jnp.arange(decode_count)[None, :])[
        None, None, None
    ]
    old_scores = (
        jnp.einsum("rtkgd,rpkd->rkgtp", queries, cache_keys, preferred_element_type=jnp.float32)
        * score_scale
    )
    old_scores = jnp.where(active_slot, old_scores, NEG_FILL)
    old_top = jnp.max(old_scores, axis=-1)
    new_scores = (
        jnp.einsum("rtkgd,rukd->rkgtu", queries, keys_new, preferred_element_type=jnp.float32)
        * score_scale
    )
    new_scores = jnp.where(causal, new_scores, NEG_FILL)
    new_top = jnp.max(new_scores, axis=-1)
    row_top = lax.pmax(jnp.maximum(old_top, new_top), "seq")
    old_weights = jnp.where(active_slot, jnp.exp(old_scores - row_top[..., None]), 0.0)
    old_total, old_pooled = lax.psum(
        (
            jnp.sum(old_weights, axis=-1),
            jnp.einsum("rkgtp,rpkd->rkgtd", old_weights, cache_values, precision=highest),
        ),
        "seq",
    )
    new_weights = jnp.where(causal, jnp.exp(new_scores - row_top[..., None]), 0.0)
    denominator = old_total + jnp.sum(new_weights, axis=-1)
    pooled = old_pooled + jnp.einsum(
        "rkgtu,rukd->rkgtd", new_weights, values_new.astype(jnp.float32), precision=highest
    )
    attended = (
        (pooled / denominator[..., None])
        .transpose(0, 3, 1, 2, 4)
        .reshape(row_count, heads_here * HD)
        .astype(jnp.bfloat16)
    )
    return lax.psum_scatter(
        jnp.dot(attended, w_out, preferred_element_type=jnp.float32).astype(jnp.bfloat16),
        "mp",
        scatter_dimension=0,
        tiled=True,
    )


def solution(mesh):
    return jax.shard_map(
        shards,
        mesh=mesh,
        in_specs=(
            P("seq", None),
            P("seq", "mp"),
            P("seq", "mp"),
            P("seq", "mp"),
            P("mp", "seq"),
            P(None, None, "seq", "mp"),
            P(),
        ),
        out_specs=P("mp", "seq"),
        check_vma=False,
    )
```

profile of v0, /device:TPU:0, one launch (start us, length us, event | category | flops | bytes accessed | tf_op | source)
XLA Modules:
  0.0 416.0 jit_solution(5943476113532040646)
XLA Ops:
  6.5 1.1 fusion.21
  7.7 1.6 fusion.22
  9.3 8.3 %all-to-all-start = ((bf16[8,16,512]{2,0,1:T(8,128)(2,1)}), bf16[8,16,512]{2,0,1:T(8,128)(2,1)S(1)}, u32[]{:S(2)}, u32[]{:S(2)}) async-start(bf16[8,16,512]{2,0,1:T(8,128)(2,1)} %bitcast), calls=%async_computation | async-start | bytes 262144 | tf_op jit(solution)/shard_map/all_to_all | solution.py:37
  17.7 7.7 %all-to-all-done = bf16[8,16,512]{2,0,1:T(8,128)(2,1)S(1)} async-done(((bf16[8,16,512]{2,0,1:T(8,128)(2,1)}), bf16[8,16,512]{2,0,1:T(8,128)(2,1)S(1)}, u32[]{:S(2)}, u32[]{:S(2)}) %all-to-all-start) | async-done | bytes 131104 | tf_op jit(solution)/shard_map/all_to_all | solution.py:37
  25.4 2.9 convolution_bitcast_fusion
  28.4 1.7 copy.37
  30.2 0.7 copy.53
  31.0 11.8 %fusion.33 = (bf16[1,32,256,512]{3,2,1,0:T(8,128)(2,1)}, bf16[1,32,256,512]{3,2,1,0:T(8,128)(2,1)}) fusion(bf16[2,32,256,512]{3,2,1,0:T(8,128)(2,1)} %param.12), kind=kLoop, calls=%fused_computation.58 | loop fusion | bytes 33554432 | tf_op jit(solution)/shard_map/slice | solution.py:64
  42.8 12.0 %copy.35 = bf16[1,32,256,512]{2,3,1,0:T(8,128)(2,1)} copy(bf16[1,32,256,512]{3,2,1,0:T(8,128)(2,1)} %get-tuple-element.10) | data formatting | bytes 16777216
  54.8 11.9 %copy.34 = bf16[1,32,256,512]{2,3,1,0:T(8,128)(2,1)} copy(bf16[1,32,256,512]{3,2,1,0:T(8,128)(2,1)} %get-tuple-element.9) | data formatting | bytes 16777216
  67.4 92.3 %all-reduce.8.cloned.1.call-done = (f32[128,32,128]{2,1,0:T(8,128)}, f32[128,4,128]{2,0,1:T(8,128)}) async-done(((f32[128,32,128]{2,1,0:T(8,128)}, f32[128,4,128]{2,0,1:T(8,128)}), (f32[128,32,128]{2,1,0:T(8,128)}, f32[128,4,128]{2,0,1:T(8,128)})) %all-reduce.8.cloned.1.call-update) | async-done | bytes 2359312 | tf_op jit(solution)/shard_map/psum | solution.py:49
  159.6 3.1 subtract_convert_fusion
  162.9 7.1 %bitcast_reduce_fusion = (f32[32,4,8,4]{2,3,1,0:T(4,128)S(1)}, f32[32,4,4,8,256]{4,3,2,1,0:T(8,128)}) fusion(pred[32,256]{1,0:T(8,128)(4,1)S(1)} %broadcast_compare_fusion, bf16[32,256,4,128,1]{1,3,4,2,0:T(8,128)(2,1)} %bitcast.63, bf16[32,4,4,8,64]{4,3,2,1,0:T(8,128)(2,1)S(1)} %bitcast.67, bf16[32,4,4,8,64]{4,3,2,1,0:T(8,128)(2,1)S(1)} %bitcast.65), kind=kOutput, calls=%fused_computation.1 | convolution fusion | flops 273674240 | bytes 13656064 | tf_op jit(solution)/shard_map/rtkgd,rpkd->rkgtp/dot_general | solution.py:73
  170.0 5.0 %fusion.34 = (f32[32,4,8,4]{2,3,1,0:T(4,128)S(1)}, f32[32,4,8,4,4]{2,4,3,1,0:T(4,128)S(1)}) fusion(pred[4,4]{1,0:T(4,128)(4,1)S(1)} %iota_compare_fusion, bf16[32,4,4,64]{3,1,0,2:T(4,128)(2,1)S(1)} %bitcast.71, bf16[32,4,4,64]{3,1,0,2:T(4,128)(2,1)S(1)} %bitcast.70, bf16[32,4,4,8,64]{4,3,2,1,0:T(8,128)(2,1)S(1)} %bitcast.68, ...), kind=kOutput, calls=%fused_computation.59 | convolution fusion | flops 6598656 | bytes 1261584 | tf_op jit(solution)/shard_map/rtkgd,rukd->rkgtu/dot_general | solution.py:79
  175.1 78.2 %pmax.7 = f32[32,4,8,4]{2,3,1,0:T(4,128)S(1)} all-reduce(f32[32,4,8,4]{2,3,1,0:T(4,128)S(1)} %max.14), channel_id=1, replica_groups=mesh['seq'=16,'mp'=2] {'seq'}, use_global_device_ids=true, to_apply=%region_5.6 | all-reduce | flops 4096 | bytes 32768 | tf_op jit(solution)/shard_map/pmax | solution.py:84
  253.3 14.2 %fusion.3 = f32[32,4,8,4,128]{4,2,3,1,0:T(8,128)} fusion(bf16[32,256,4,128,1]{1,3,4,2,0:T(8,128)(2,1)} %bitcast.62, f32[32,4,4,8,256]{4,3,2,1,0:T(8,128)} %get-tuple-element.18, f32[32,4,8,4]{2,3,1,0:T(4,128)S(1)} %pmax.7, pred[32,256]{1,0:T(8,128)(4,1)S(1)} %broadcast_compare_fusion), kind=kOutput, calls=%fused_computation.6 | convolution fusion | flops 1614807040 | bytes 14704640 | tf_op jit(solution)/shard_map/rkgtp,rpkd->rkgtd/dot_general | solution.py:89
  267.8 3.6 fusion.2
  271.4 81.3 %all-reduce.9 = (f32[32,4,8,4]{2,3,1,0:T(4,128)S(1)}, bf16[128,512]{1,0:T(8,128)(2,1)S(1)}) all-reduce(f32[32,4,8,4]{2,3,1,0:T(4,128)S(1)} %fusion.2, f32[128,512]{1,0:T(8,128)S(1)} %fusion.25), channel_id=1, replica_groups=mesh['seq'=16,'mp'=2] {'seq'}, use_global_device_ids=true, to_apply=%region_9.10 | all-reduce | flops 69632 | bytes 425984 | tf_op jit(solution)/shard_map/psum | solution.py:86
  352.7 1.0 fusion.17
  353.8 40.5 %all-reduce.6.cloned.1.call-done = f32[32,4,8,4,128]{4,2,3,1,0:T(8,128)} async-done(((f32[32,4,8,4,128]{4,2,3,1,0:T(8,128)}), f32[32,4,8,4,128]{4,2,3,1,0:T(8,128)}) %all-reduce.6.cloned.1.call-update) | async-done | bytes 2097168 | tf_op jit(solution)/shard_map/psum | solution.py:86
  394.4 3.8 fusion.11
  398.4 0.5 convert_element_type.47
  398.9 3.5 convolution_convert_fusion
  402.5 7.0 %reduce-scatter.2.cloned.1.call-done = bf16[64,512]{1,0:T(8,128)(2,1)} async-done(((bf16[128,512]{1,0:T(8,128)(2,1)}), bf16[64,512]{1,0:T(8,128)(2,1)}) %reduce-scatter.2.cloned.1.call-update) | async-done | bytes 65552 | tf_op jit(solution)/shard_map/reduce_scatter | solution.py:104
  (31 shorter events, 1.8 us)
Async XLA Ops:
  6.5 23.5 %copy-start = (bf16[512,512]{1,0:T(8,128)(2,1)S(1)}, bf16[512,512]{1,0:T(8,128)(2,1)}, u32[]{:S(2)}) copy-start(bf16[512,512]{1,0:T(8,128)(2,1)} %param.9) | copy-start | bytes 1572868
  9.3 16.1 %all-to-all-start = ((bf16[8,16,512]{2,0,1:T(8,128)(2,1)}), bf16[8,16,512]{2,0,1:T(8,128)(2,1)S(1)}, u32[]{:S(2)}, u32[]{:S(2)}) async-start(bf16[8,16,512]{2,0,1:T(8,128)(2,1)} %bitcast), calls=%async_computation | async-start | bytes 262144 | tf_op jit(solution)/shard_map/all_to_all | solution.py:37
  17.6 142.0 %all-reduce.8.cloned.1.call-start = ((), (), s32[]{:S(2)}) async-start(), calls=%async_computation.4 | async-start | bytes 4718592 | tf_op jit(solution)/shard_map/psum | solution.py:49
  31.0 363.4 %all-reduce.6.cloned.1.call-start = ((), (), s32[]{:S(2)}) async-start(), calls=%async_computation.2 | async-start | bytes 4194304 | tf_op jit(solution)/shard_map/psum | solution.py:86
  54.8 11.9 %copy-start.4 = (s32[32]{0:T(128)S(1)}, s32[32]{0:T(128)}, u32[]{:S(2)}) copy-start(s32[32]{0:T(128)} %param.13) | copy-start | bytes 388
  159.6 3.1 copy-start.2
  253.3 14.3 %copy-start.3 = (bf16[512,512]{1,0:T(8,128)(2,1)S(1)}, bf16[512,512]{1,0:T(8,128)(2,1)}, u32[]{:S(2)}) copy-start(bf16[512,512]{1,0:T(8,128)(2,1)} %param.10) | copy-start | bytes 1572868
  267.5 142.0 %reduce-scatter.2.cloned.1.call-start = ((), (), s32[]{:S(2)}) async-start(), calls=%async_computation.3 | async-start | bytes 196608 | tf_op jit(solution)/shard_map/reduce_scatter | solution.py:104
  398.2 11.3 %copy-start.1 = (bf16[512,512]{1,0:T(8,128)(2,1)S(1)}, bf16[512,512]{1,0:T(8,128)(2,1)}, u32[]{:S(2)}) copy-start(bf16[512,512]{1,0:T(8,128)(2,1)} %param.9) | copy-start | bytes 1572868
Sparse Core Ops, SparseCore 0:
  31.1 128.4 all-reduce.7
  267.6 126.7 all-reduce.5
  402.6 6.8 reduce-scatter.1
where the time goes:
time: 417 us; the launch traced here: 416 us
  blocking collectives  159 us (38%)
  waiting for transfers between devices  148 us (35%)
  local copies, waits for them, and re-layouts  38.9 us (9%)
  matrix products  37.1 us (9%)
  between operations  13.3 us (3%)
  other arithmetic  11.3 us (3%)
  starting transfers between devices  8.44 us (2%)
    psum x1, waiting for transfers between devices, shards(): lax.psum((partial_query, partial_key, partial_value), 'seq')  92.3 us
    psum x1, blocking collectives, shards(): lax.psum((jnp.sum(old_weights, axis=-1), jnp.einsum('rkgtp,rpkd->rkgtd',...  81.3 us
    pmax x1, blocking collectives, shards(): row_top = lax.pmax(jnp.maximum(old_top, new_top), 'seq')  78.2 us
    psum x1, waiting for transfers between devices, shards(): lax.psum((jnp.sum(old_weights, axis=-1), jnp.einsum('rkgtp,rpkd->rkgtd',...  40.5 us
    unnamed x13, local copies, waits for them, and re-layouts  25.6 us
    dot_general x1, matrix products, shards(): jnp.einsum('rkgtp,rpkd->rkgtd', old_weights, cache_values, precision=high...  14.2 us
    slice x1, local copies, waits for them, and re-layouts, shards(): cache_keys = kv_cache[0].reshape(request_count, block_size, kv_here, HD)  11.8 us
  transfers between devices with their start and end apart: 4, of which 4 were waited for; matrix products, arithmetic and copies ran while one was open for 10% of the time, Pallas kernels for 0%

commit v1 on v0

--- a/solution.py
+++ b/solution.py
@@ -34,7 +34,10 @@
     normed = (
         widened * lax.rsqrt(jnp.mean(widened * widened, axis=-1, keepdims=True) + 1e-05)
     ).astype(jnp.bfloat16)
-    gathered = lax.all_to_all(normed, "seq", split_axis=1, concat_axis=0, tiled=True)
+    gathered = jnp.concatenate(
+        lax.all_to_all(jnp.stack(jnp.split(normed, lax.axis_size("seq"), axis=1)), "seq", 0, 0),
+        axis=0,
+    )
     partial_query = jnp.dot(gathered, w_query, preferred_element_type=jnp.float32)
     partial_key = jnp.dot(gathered, w_key, preferred_element_type=jnp.float32)
     partial_value = jnp.dot(gathered, w_value, preferred_element_type=jnp.float32)

time: 417 us -> 426 us (1.022)
  local copies, waits for them, and re-layouts: 38.9 us -> 48.4 us
    unnamed x13 -> x28, local copies, waits for them, and re-layouts: 25.6 us -> 34.5 us
where the time goes in v1:
time: 426 us; the launch traced here: 425 us
  blocking collectives  159 us (37%)
  waiting for transfers between devices  148 us (35%)
  local copies, waits for them, and re-layouts  48.4 us (11%)
  matrix products  37 us (9%)
  between operations  13.3 us (3%)
  other arithmetic  10.6 us (2%)
  starting transfers between devices  8.44 us (2%)
    psum x1, waiting for transfers between devices, shards(): lax.psum((partial_query, partial_key, partial_value), 'seq')  92.3 us
    psum x1, blocking collectives, shards(): lax.psum((jnp.sum(old_weights, axis=-1), jnp.einsum('rkgtp,rpkd->rkgtd',...  81.2 us
    pmax x1, blocking collectives, shards(): row_top = lax.pmax(jnp.maximum(old_top, new_top), 'seq')  78.2 us
    psum x1, waiting for transfers between devices, shards(): lax.psum((jnp.sum(old_weights, axis=-1), jnp.einsum('rkgtp,rpkd->rkgtd',...  40.7 us
    unnamed x28, local copies, waits for them, and re-layouts  34.5 us
    dot_general x1, matrix products, shards(): jnp.einsum('rkgtp,rpkd->rkgtd', old_weights, cache_values, precision=high...  14.2 us
    slice x1, local copies, waits for them, and re-layouts, shards(): cache_keys = kv_cache[0].reshape(request_count, block_size, kv_here, HD)  11.8 us
  transfers between devices with their start and end apart: 4, of which 4 were waited for; matrix products, arithmetic and copies ran while one was open for 10% of the time, Pallas kernels for 0%

profile of v1, /device:TPU:0, one launch (start us, length us, event | category | flops | bytes accessed | tf_op | source)
XLA Modules:
  0.0 425.0 jit_solution(13864793072364935634)
XLA Ops:
  6.5 1.1 fusion.21
  7.7 1.0 fusion.22
  17.0 0.6 constant_dynamic-update-slice_fusion.1
  18.2 8.3 %all-to-all-start = ((bf16[16,8,512]{2,1,0:T(8,128)(2,1)}), bf16[16,8,512]{2,1,0:T(8,128)(2,1)S(1)}, u32[]{:S(2)}, u32[]{:S(2)}) async-start(bf16[16,8,512]{2,1,0:T(8,128)(2,1)} %constant_dynamic-update-slice_fusion), calls=%async_computation | async-start | bytes 262144 | tf_op jit(solution)/shard_map/all_to_all | solution.py:38
  26.6 7.7 %all-to-all-done = bf16[16,8,512]{2,1,0:T(8,128)(2,1)S(1)} async-done(((bf16[16,8,512]{2,1,0:T(8,128)(2,1)}), bf16[16,8,512]{2,1,0:T(8,128)(2,1)S(1)}, u32[]{:S(2)}, u32[]{:S(2)}) %all-to-all-start) | async-done | bytes 131104 | tf_op jit(solution)/shard_map/all_to_all | solution.py:38
  34.3 2.9 convolution_bitcast_fusion
  37.2 1.7 copy.37
  39.1 0.7 copy.53
  39.9 11.8 %fusion.33 = (bf16[1,32,256,512]{3,2,1,0:T(8,128)(2,1)}, bf16[1,32,256,512]{3,2,1,0:T(8,128)(2,1)}) fusion(bf16[2,32,256,512]{3,2,1,0:T(8,128)(2,1)} %param.12), kind=kLoop, calls=%fused_computation.90 | loop fusion | bytes 33554432 | tf_op jit(solution)/shard_map/slice | solution.py:67
  51.7 12.0 %copy.35 = bf16[1,32,256,512]{2,3,1,0:T(8,128)(2,1)} copy(bf16[1,32,256,512]{3,2,1,0:T(8,128)(2,1)} %get-tuple-element.10) | data formatting | bytes 16777216
  63.7 11.9 %copy.34 = bf16[1,32,256,512]{2,3,1,0:T(8,128)(2,1)} copy(bf16[1,32,256,512]{3,2,1,0:T(8,128)(2,1)} %get-tuple-element.9) | data formatting | bytes 16777216
  76.2 92.3 %all-reduce.8.cloned.1.call-done = (f32[128,32,128]{2,1,0:T(8,128)}, f32[128,4,128]{2,0,1:T(8,128)}) async-done(((f32[128,32,128]{2,1,0:T(8,128)}, f32[128,4,128]{2,0,1:T(8,128)}), (f32[128,32,128]{2,1,0:T(8,128)}, f32[128,4,128]{2,0,1:T(8,128)})) %all-reduce.8.cloned.1.call-update) | async-done | bytes 2359312 | tf_op jit(solution)/shard_map/psum | solution.py:52
  168.5 3.1 subtract_convert_fusion
  171.7 7.1 %bitcast_reduce_fusion = (f32[32,4,8,4]{2,3,1,0:T(4,128)S(1)}, f32[32,4,4,8,256]{4,3,2,1,0:T(8,128)}) fusion(pred[32,256]{1,0:T(8,128)(4,1)S(1)} %broadcast_compare_fusion, bf16[32,256,4,128,1]{1,3,4,2,0:T(8,128)(2,1)} %bitcast.124, bf16[32,4,4,8,64]{4,3,2,1,0:T(8,128)(2,1)S(1)} %bitcast.128, bf16[32,4,4,8,64]{4,3,2,1,0:T(8,128)(2,1)S(1)} %bitcast.126), kind=kOutput, calls=%fused_computation.1 | convolution fusion | flops 273674240 | bytes 13656064 | tf_op jit(solution)/shard_map/rtkgd,rpkd->rkgtp/dot_general | solution.py:76
  178.9 5.0 %fusion.34 = (f32[32,4,8,4]{2,3,1,0:T(4,128)S(1)}, f32[32,4,8,4,4]{2,4,3,1,0:T(4,128)S(1)}) fusion(pred[4,4]{1,0:T(4,128)(4,1)S(1)} %iota_compare_fusion, bf16[32,4,4,64]{3,1,0,2:T(4,128)(2,1)S(1)} %bitcast.132, bf16[32,4,4,64]{3,1,0,2:T(4,128)(2,1)S(1)} %bitcast.131, bf16[32,4,4,8,64]{4,3,2,1,0:T(8,128)(2,1)S(1)} %bitcast.129, ...), kind=kOutput, calls=%fused_computation.91 | convolution fusion | flops 6598656 | bytes 1261584 | tf_op jit(solution)/shard_map/rtkgd,rukd->rkgtu/dot_general | solution.py:82
  184.0 78.2 %pmax.7 = f32[32,4,8,4]{2,3,1,0:T(4,128)S(1)} all-reduce(f32[32,4,8,4]{2,3,1,0:T(4,128)S(1)} %max.14), channel_id=1, replica_groups=mesh['seq'=16,'mp'=2] {'seq'}, use_global_device_ids=true, to_apply=%region_5.6 | all-reduce | flops 4096 | bytes 32768 | tf_op jit(solution)/shard_map/pmax | solution.py:87
  262.2 14.2 %fusion.3 = f32[32,4,8,4,128]{4,2,3,1,0:T(8,128)} fusion(bf16[32,256,4,128,1]{1,3,4,2,0:T(8,128)(2,1)} %bitcast.123, f32[32,4,4,8,256]{4,3,2,1,0:T(8,128)} %get-tuple-element.18, f32[32,4,8,4]{2,3,1,0:T(4,128)S(1)} %pmax.7, pred[32,256]{1,0:T(8,128)(4,1)S(1)} %broadcast_compare_fusion), kind=kOutput, calls=%fused_computation.6 | convolution fusion | flops 1614807040 | bytes 14704640 | tf_op jit(solution)/shard_map/rkgtp,rpkd->rkgtd/dot_general | solution.py:92
  276.7 3.6 fusion.2
  280.3 81.2 %all-reduce.9 = (f32[32,4,8,4]{2,3,1,0:T(4,128)S(1)}, bf16[128,512]{1,0:T(8,128)(2,1)S(1)}) all-reduce(f32[32,4,8,4]{2,3,1,0:T(4,128)S(1)} %fusion.2, f32[128,512]{1,0:T(8,128)S(1)} %fusion.25), channel_id=1, replica_groups=mesh['seq'=16,'mp'=2] {'seq'}, use_global_device_ids=true, to_apply=%region_9.10 | all-reduce | flops 69632 | bytes 425984 | tf_op jit(solution)/shard_map/psum | solution.py:89
  361.5 1.0 fusion.17
  362.6 40.7 %all-reduce.6.cloned.1.call-done = f32[32,4,8,4,128]{4,2,3,1,0:T(8,128)} async-done(((f32[32,4,8,4,128]{4,2,3,1,0:T(8,128)}), f32[32,4,8,4,128]{4,2,3,1,0:T(8,128)}) %all-reduce.6.cloned.1.call-update) | async-done | bytes 2097168 | tf_op jit(solution)/shard_map/psum | solution.py:89
  403.3 3.8 fusion.11
  407.9 3.6 convolution_convert_fusion
  411.4 7.0 %reduce-scatter.2.cloned.1.call-done = bf16[64,512]{1,0:T(8,128)(2,1)} async-done(((bf16[128,512]{1,0:T(8,128)(2,1)}), bf16[64,512]{1,0:T(8,128)(2,1)}) %reduce-scatter.2.cloned.1.call-update) | async-done | bytes 65552 | tf_op jit(solution)/shard_map/reduce_scatter | solution.py:107
  (47 shorter events, 11.2 us)
Async XLA Ops:
  6.5 32.4 %copy-start = (bf16[512,512]{1,0:T(8,128)(2,1)S(1)}, bf16[512,512]{1,0:T(8,128)(2,1)}, u32[]{:S(2)}) copy-start(bf16[512,512]{1,0:T(8,128)(2,1)} %param.9) | copy-start | bytes 1572868
  18.2 16.1 %all-to-all-start = ((bf16[16,8,512]{2,1,0:T(8,128)(2,1)}), bf16[16,8,512]{2,1,0:T(8,128)(2,1)S(1)}, u32[]{:S(2)}, u32[]{:S(2)}) async-start(bf16[16,8,512]{2,1,0:T(8,128)(2,1)} %constant_dynamic-update-slice_fusion), calls=%async_computation | async-start | bytes 262144 | tf_op jit(solution)/shard_map/all_to_all | solution.py:38
  26.5 142.0 %all-reduce.8.cloned.1.call-start = ((), (), s32[]{:S(2)}) async-start(), calls=%async_computation.4 | async-start | bytes 4718592 | tf_op jit(solution)/shard_map/psum | solution.py:52
  39.9 363.4 %all-reduce.6.cloned.1.call-start = ((), (), s32[]{:S(2)}) async-start(), calls=%async_computation.2 | async-start | bytes 4194304 | tf_op jit(solution)/shard_map/psum | solution.py:89
  63.7 11.9 %copy-start.4 = (s32[32]{0:T(128)S(1)}, s32[32]{0:T(128)}, u32[]{:S(2)}) copy-start(s32[32]{0:T(128)} %param.13) | copy-start | bytes 388
  168.5 3.1 copy-start.2
  262.2 14.3 %copy-start.3 = (bf16[512,512]{1,0:T(8,128)(2,1)S(1)}, bf16[512,512]{1,0:T(8,128)(2,1)}, u32[]{:S(2)}) copy-start(bf16[512,512]{1,0:T(8,128)(2,1)} %param.10) | copy-start | bytes 1572868
  276.4 142.1 %reduce-scatter.2.cloned.1.call-start = ((), (), s32[]{:S(2)}) async-start(), calls=%async_computation.3 | async-start | bytes 196608 | tf_op jit(solution)/shard_map/reduce_scatter | solution.py:107
  407.1 11.3 %copy-start.1 = (bf16[512,512]{1,0:T(8,128)(2,1)S(1)}, bf16[512,512]{1,0:T(8,128)(2,1)}, u32[]{:S(2)}) copy-start(bf16[512,512]{1,0:T(8,128)(2,1)} %param.9) | copy-start | bytes 1572868
Sparse Core Ops, SparseCore 0:
  40.0 128.4 all-reduce.7
  276.5 126.7 all-reduce.5
  411.6 6.8 reduce-scatter.1
